TPU v7x, 32 devices: a whole 2x2x4 slice. The times are simulated.
32 devices in a mesh: replica: 8 (over z, y), tp: 4 (over x, core).
Axes of the slice: x: 2, y: 2, z: 4, core: 2. Of those that a mesh axis runs over, the one named last changes fastest.
Arguments:
- hidden: bfloat16 [96, 4, 8192], P('replica', None, 'tp'), may hold values from -6 to 6
- norm_gain: float32 [8192], replicated, may hold values from 0.5 to 1.5
- w_query: float32 [8192, 4096], P(('replica', 'tp')), may hold values from -0.0625 to 0.0625
- w_key: float32 [8192, 512], P(('replica', 'tp')), may hold values from -0.0625 to 0.0625
- w_value: float32 [8192, 512], P(('replica', 'tp')), may hold values from -0.0625 to 0.0625
- bias_query: float32 [4096], P('tp'), may hold values from -3 to 3
- bias_key: float32 [512], P('tp'), may hold values from -3 to 3
- bias_value: float32 [512], P('tp'), may hold values from -3 to 3
- key_pages: bfloat16 [512, 4, 128, 128], P(('replica', 'tp')), may hold values from -256 to 256
- value_pages: bfloat16 [512, 4, 128, 128], P(('replica', 'tp')), may hold values from -6 to 6
- kv_lengths: int32 [96], P(('replica', 'tp')), may hold values from 1 to 1024, as said below
- page_table: int32 [96, 8], P(('replica', 'tp')), may hold values from 0 to 15, as said below
Outputs:
- attended: bfloat16 [96, 4, 4096], P(('replica', 'tp'))
Inputs may be any that keep to these rules, and one draw needn't show every extreme that they name: `kv_lengths`: on every device, one row has exactly 1024 cached tokens. `page_table`: page ids are local to the pool of 16 pages of the device that holds the row. The first ceil(kv_lengths / 128) entries of a row name its pages in order; no page serves two of those entries on one device; later entries are arbitrary pages of the pool.
All inputs are finite; a program needn't handle non-finite values.
Results may differ from a plain program's by a relative error of at most 0.04.
Values may be sent and summed in bfloat16 or wider, within the bound.
No kernel may reach another device: no remote copies, remote signals or barrier semaphores. Data moves between devices by JAX's collectives and lax.ppermute only.
A program may use at most 128 MiB of HBM per device.

v0:
```python
import jax
import jax.numpy as jnp
from jax import lax
from jax.sharding import PartitionSpec as P

HD = 128
HQ = 32
KVH = 4
PAGE = 128
MOSTP = 8
EPS = 1e-06
THETA = 1000000.0


def rotate(values, positions):
    half = values.shape[-1] // 2
    freq = THETA ** (-(jnp.arange(half, dtype=jnp.float32) * 2.0 / values.shape[-1]))
    angle = positions.astype(jnp.float32)[..., None] * freq
    angle = jnp.concatenate([angle, angle], -1)[:, :, None, :]
    turned = jnp.concatenate([-values[..., half:], values[..., :half]], -1)
    return values * jnp.cos(angle) + turned * jnp.sin(angle)


def on_device(
    hidden,
    norm_gain,
    w_query,
    w_key,
    w_value,
    bias_query,
    bias_key,
    bias_value,
    key_pages,
    value_pages,
    kv_lengths,
    page_table,
):
    shards = (
        w_query.astype(jnp.bfloat16),
        w_key.astype(jnp.bfloat16),
        w_value.astype(jnp.bfloat16),
    )
    whole = lax.all_gather(hidden, "tp", axis=2, tiled=True)
    count, steps, width = whole.shape
    wide = whole.astype(jnp.float32)
    power = jnp.mean(wide * wide, axis=2, keepdims=True)
    normed = (
        (wide * lax.rsqrt(power + EPS) * norm_gain)
        .astype(jnp.bfloat16)
        .reshape(count * steps, width)
    )
    local = (
        lax.all_to_all(shards[0], "tp", split_axis=1, concat_axis=0, tiled=True),
        lax.all_to_all(shards[1], "tp", split_axis=1, concat_axis=0, tiled=True),
        lax.all_to_all(shards[2], "tp", split_axis=1, concat_axis=0, tiled=True),
    )
    pieces = (
        lax.all_gather(local[0], "replica", axis=0, tiled=True),
        lax.all_gather(local[1], "replica", axis=0, tiled=True),
        lax.all_gather(local[2], "replica", axis=0, tiled=True),
    )
    sums = tuple((jnp.dot(normed, piece, preferred_element_type=jnp.float32) for piece in pieces))
    made = [
        (total + bias).astype(jnp.bfloat16).reshape(count, steps, -1)
        for total, bias in zip(sums, (bias_query, bias_key, bias_value))
    ]
    query, key_new, value_new = (
        lax.all_to_all(made[0], "tp", split_axis=0, concat_axis=2, tiled=True),
        lax.all_to_all(made[1], "tp", split_axis=0, concat_axis=2, tiled=True),
        lax.all_to_all(made[2], "tp", split_axis=0, concat_axis=2, tiled=True),
    )
    rows = query.shape[0]
    steps = query.shape[1]
    query = query.reshape(rows, steps, HQ, HD)
    key_new = key_new.reshape(rows, steps, KVH, HD)
    value_new = value_new.reshape(rows, steps, KVH, HD)
    positions = kv_lengths[:, None] + jnp.arange(steps, dtype=jnp.int32)[None, :]
    query_rot = rotate(query.astype(jnp.float32), positions).astype(jnp.bfloat16)
    key_rot = rotate(key_new.astype(jnp.float32), positions).astype(jnp.bfloat16)
    group = HQ // KVH
    scale = 1.0 / HD**0.5
    q_heads = query_rot.reshape(rows, steps, KVH, group, HD)
    keys = jnp.take(key_pages, page_table, axis=0)
    vals = jnp.take(value_pages, page_table, axis=0)
    cache = (
        jnp.einsum("rtkgd,rmknd->rtkgmn", q_heads, keys, preferred_element_type=jnp.float32) * scale
    )
    spot = jnp.arange(MOSTP)[:, None] * PAGE + jnp.arange(PAGE)[None, :]
    live = (spot[None] < kv_lengths[:, None, None])[:, None, None, None]
    cache = jnp.where(live, cache, -1e30)
    causal = jnp.arange(steps)[None, :] <= jnp.arange(steps)[:, None]
    fresh = (
        jnp.einsum("rtkgd,rskd->rtkgs", q_heads, key_rot, preferred_element_type=jnp.float32)
        * scale
    )
    fresh = jnp.where(causal[None, :, None, None, :], fresh, -1e30)
    top = jnp.maximum(jnp.max(cache, axis=(4, 5)), jnp.max(fresh, axis=4))
    e_cache = jnp.where(live, jnp.exp(cache - top[..., None, None]), 0.0)
    e_fresh = jnp.where(causal[None, :, None, None, :], jnp.exp(fresh - top[..., None]), 0.0)
    total = jnp.sum(e_cache, axis=(4, 5)) + jnp.sum(e_fresh, axis=4)
    w_cache = (e_cache / total[..., None, None]).astype(jnp.bfloat16)
    w_fresh = (e_fresh / total[..., None]).astype(jnp.bfloat16)
    out = jnp.einsum("rtkgmn,rmknd->rtkgd", w_cache, vals, preferred_element_type=jnp.float32)
    out = out + jnp.einsum(
        "rtkgs,rskd->rtkgd", w_fresh, value_new, preferred_element_type=jnp.float32
    )
    return out.reshape(rows, steps, HQ * HD).astype(jnp.bfloat16)


def solution(mesh):
    in_specs = (
        P("replica", None, "tp"),
        P(),
        P(("replica", "tp"), None),
        P(("replica", "tp"), None),
        P(("replica", "tp"), None),
        P("tp"),
        P("tp"),
        P("tp"),
        P(("replica", "tp"), None, None, None),
        P(("replica", "tp"), None, None, None),
        P(("replica", "tp")),
        P(("replica", "tp"), None),
    )
    out_specs = P(("replica", "tp"), None, None)
    return jax.shard_map(
        on_device, mesh=mesh, in_specs=in_specs, out_specs=out_specs, check_vma=False
    )
```

profile of v0, /device:TPU:0, one launch (start us, length us, event | category | flops | bytes accessed | tf_op | source)
XLA Modules:
  0.0 380.4 jit_solution(5661806267189946849)
XLA Ops:
  6.5 1.3 copy.32
  7.9 10.0 %all_to_all.90 = bf16[256,4,128]{0,2,1:T(8,128)(2,1)S(1)} all-to-all(bf16[256,4,128]{0,2,1:T(8,128)(2,1)S(1)} %bitcast.101), channel_id=1, replica_groups=mesh['replica'=8,'tp'=4] {'tp'}, dimensions={1} | all-to-all | bytes 524288 | tf_op jit(solution)/shard_map/all_to_all | solution.py:54
  17.9 0.8 copy.33
  19.0 8.4 %all_to_all.91 = bf16[256,4,128]{0,2,1:T(8,128)(2,1)S(1)} all-to-all(bf16[256,4,128]{0,2,1:T(8,128)(2,1)S(1)} %bitcast.102), channel_id=1, replica_groups=mesh['replica'=8,'tp'=4] {'tp'}, dimensions={1} | all-to-all | bytes 524288 | tf_op jit(solution)/shard_map/all_to_all | solution.py:55
  27.4 0.9 copy.38
  28.3 4.6 %copy.27 = bf16[256,4096]{0,1:T(8,128)(2,1)} copy(f32[256,4096]{1,0:T(8,128)} %param.16) | data formatting | bytes 6291456 | tf_op args[2]
  32.9 30.1 %all_to_all.92 = bf16[256,4,1024]{0,2,1:T(8,128)(2,1)} all-to-all(bf16[256,4,1024]{0,2,1:T(8,128)(2,1)} %bitcast.96), channel_id=1, replica_groups=mesh['replica'=8,'tp'=4] {'tp'}, dimensions={1} | all-to-all | bytes 4194304 | tf_op jit(solution)/shard_map/all_to_all | solution.py:53
  63.1 4.0 %copy.28 = bf16[4,256,1024]{2,1,0:T(8,128)(2,1)} copy(bf16[4,256,1024]{1,2,0:T(8,128)(2,1)} %bitcast.98) | data formatting | bytes 4194304 | tf_op jit(solution)/shard_map/all_to_all | solution.py:53
  67.1 0.9 copy-done.3
  68.0 7.8 %all_gather.12 = bf16[12,4,8192]{2,1,0:T(4,128)(2,1)S(1)} all-gather(bf16[12,4,2048]{2,1,0:T(4,128)(2,1)S(1)} %copy-done.3), channel_id=1, replica_groups=mesh['replica'=8,'tp'=4] {'tp'}, dimensions={2}, use_global_device_ids=true | all-gather | bytes 983040 | tf_op jit(solution)/shard_map/all_gather | solution.py:43
  75.8 0.5 fusion.6
  76.3 1.4 fusion.8
  77.7 1.6 reshape.170
  79.4 2.7 gather_fusion.1
  82.2 4.3 %gather_fusion = bf16[24,4,128,128]{3,2,1,0:T(8,128)(2,1)} fusion(bf16[16,4,128,128]{3,2,1,0:T(8,128)(2,1)} %param.23, s32[1024]{0:T(1024)S(1)} %pad_clamp_fusion), kind=kCustom, calls=%fused_computation.clone | custom fusion | bytes 6291552 | tf_op jit(solution)/shard_map/jit(_take)/gather | solution.py:84
  87.0 2.7 fusion.24
  89.6 3.4 all-to-all-start.3
  93.0 25.1 %all-gather.8.cloned.1.call-done = bf16[8192,128]{1,0:T(8,128)(2,1)} async-done(((bf16[1024,128]{1,0:T(8,128)(2,1)}), bf16[8192,128]{1,0:T(8,128)(2,1)}) %all-gather.8.cloned.1.call-update) | async-done | bytes 2097168 | tf_op jit(solution)/shard_map/all_gather | solution.py:60
  118.2 2.7 fusion.25
  120.8 225.3 %all-gather.4.cloned.1.call-done = bf16[8192,1024]{1,0:T(8,128)(2,1)} async-done(((bf16[1024,1024]{1,0:T(8,128)(2,1)}), bf16[8192,1024]{1,0:T(8,128)(2,1)}) %all-gather.4.cloned.1.call-update) | async-done | bytes 16777232 | tf_op jit(solution)/shard_map/all_gather | solution.py:58
  346.1 8.8 %fusion.19 = bf16[48,1024]{1,0:T(8,128)(2,1)S(1)} fusion(bf16[48,8192]{1,0:T(8,128)(2,1)S(1)} %reshape.170, bf16[8192,1024]{1,0:T(8,128)(2,1)} %all-gather.4.cloned.1.call-done, f32[1024]{0:T(1024)S(1)} %copy-done.6), kind=kOutput, calls=%fused_computation.27 | convolution fusion | flops 805404672 | bytes 17666048 | tf_op jit(solution)/shard_map/dot_general | solution.py:62
  354.9 0.7 reshape.171
  355.6 3.3 all-to-all-start.1
  359.0 4.2 %all-to-all-done.1 = bf16[12,4,1024]{2,1,0:T(4,128)(2,1)S(1)} async-done(((bf16[12,4,1024]{2,1,0:T(4,128)(2,1)}), bf16[12,4,1024]{2,1,0:T(4,128)(2,1)S(1)}, u32[]{:S(2)}, u32[]{:S(2)}) %all-to-all-start.1) | async-done | bytes 98336 | tf_op jit(solution)/shard_map/all_to_all | solution.py:68
  363.2 3.4 all-to-all-start.5
  367.2 0.6 fusion.52
  367.8 3.4 bitcast_reduce_fusion
  371.2 0.2 fusion.35
  371.4 0.4 fusion.15
  371.8 1.0 fusion.16
  372.8 0.3 fusion.21
  373.2 0.7 convert_element_type.107
  (53 shorter events, 1.5 us)
Async XLA Ops:
  6.5 72.9 %copy-start = (bf16[16,4,128,128]{3,2,1,0:T(8,128)(2,1)S(1)}, bf16[16,4,128,128]{3,2,1,0:T(8,128)(2,1)}, u32[]{:S(2)}) copy-start(bf16[16,4,128,128]{3,2,1,0:T(8,128)(2,1)} %param.22) | copy-start | bytes 6291460
  6.5 12.3 %copy-start.2 = (f32[256,512]{1,0:T(8,128)S(1)}, f32[256,512]{1,0:T(8,128)}, u32[]{:S(2)}) copy-start(f32[256,512]{1,0:T(8,128)} %param.18) | copy-start | bytes 1572868
  6.5 80.4 %all-gather.6.cloned.1.call-start = ((), (), s32[]{:S(2)}) async-start(), calls=%async_computation.7 | async-start | bytes 2359296 | tf_op jit(solution)/shard_map/all_gather | solution.py:59
  18.8 99.4 %all-gather.8.cloned.1.call-start = ((), (), s32[]{:S(2)}) async-start(), calls=%async_computation.8 | async-start | bytes 2359296 | tf_op jit(solution)/shard_map/all_gather | solution.py:60
  28.3 317.9 %all-gather.4.cloned.1.call-start = ((), (), s32[]{:S(2)}) async-start(), calls=%async_computation.6 | async-start | bytes 18874368 | tf_op jit(solution)/shard_map/all_gather | solution.py:58
  67.0 0.9 copy-start.3
  67.0 9.3 %copy-start.4 = (f32[8192]{0:T(1024)S(1)}, f32[8192]{0:T(1024)}, u32[]{:S(2)}) copy-start(f32[8192]{0:T(1024)} %param.15) | copy-start | bytes 98308
  75.8 3.5 copy-start.5
  82.2 4.4 %copy-start.7 = (s32[3]{0:T(128)S(1)}, s32[3]{0:T(128)}, u32[]{:S(2)}) copy-start(s32[3]{0:T(128)} %param.24) | copy-start | bytes 40
  82.2 4.8 %copy-start.8 = (f32[128]{0:T(128)S(1)}, f32[128]{0:T(128)}, u32[]{:S(2)}) copy-start(f32[128]{0:T(128)} %param.20) | copy-start | bytes 1540
  86.5 31.7 %copy-start.9 = (f32[128]{0:T(128)S(1)}, f32[128]{0:T(128)}, u32[]{:S(2)}) copy-start(f32[128]{0:T(128)} %param.21) | copy-start | bytes 1540
  89.6 256.5 %copy-start.6 = (f32[1024]{0:T(1024)S(1)}, f32[1024]{0:T(1024)}, u32[]{:S(2)}) copy-start(f32[1024]{0:T(1024)} %param.19) | copy-start | bytes 12292
  89.6 31.2 %all-to-all-start.3 = ((bf16[12,4,128]{2,1,0:T(4,128)(2,1)}), bf16[12,4,128]{2,1,0:T(4,128)(2,1)S(1)}, u32[]{:S(2)}, u32[]{:S(2)}) async-start(bf16[12,4,128]{2,1,0:T(4,128)(2,1)} %bitcast.19), calls=%async_computation.3 | async-start | bytes 24576 | tf_op jit(solution)/shard_map/all_to_all | solution.py:69
  355.6 7.6 %all-to-all-start.1 = ((bf16[12,4,1024]{2,1,0:T(4,128)(2,1)}), bf16[12,4,1024]{2,1,0:T(4,128)(2,1)S(1)}, u32[]{:S(2)}, u32[]{:S(2)}) async-start(bf16[12,4,1024]{2,1,0:T(4,128)(2,1)} %reshape.171), calls=%async_computation.1 | async-start | bytes 196608 | tf_op jit(solution)/shard_map/all_to_all | solution.py:68
  363.2 9.6 %all-to-all-start.5 = ((bf16[12,4,128]{2,1,0:T(4,128)(2,1)}), bf16[12,4,128]{2,1,0:T(4,128)(2,1)S(1)}, u32[]{:S(2)}, u32[]{:S(2)}) async-start(bf16[12,4,128]{2,1,0:T(4,128)(2,1)} %bitcast.30), calls=%async_computation.5 | async-start | bytes 24576 | tf_op jit(solution)/shard_map/all_to_all | solution.py:70
  367.8 4.0 %copy-start.1 = (bf16[24,4,128,128]{3,2,1,0:T(8,128)(2,1)S(1)}, bf16[24,4,128,128]{3,2,1,0:T(8,128)(2,1)}, u32[]{:S(2)}) copy-start(bf16[24,4,128,128]{3,2,1,0:T(8,128)(2,1)} %gather_fusion) | copy-start | bytes 9437188
Sparse Core Ops, SparseCore 0:
  18.9 49.3 all-gather.5
  70.5 47.6 all-gather.7
  120.3 225.7 all-gather.3
where the time goes:
time: 381 us; the launch traced here: 380 us
  waiting for transfers between devices  255 us (67%)
  blocking collectives  56.4 us (15%)
  local copies, waits for them, and re-layouts  23.1 us (6%)
  matrix products  19.4 us (5%)
  between operations  13.4 us (4%)
  starting transfers between devices  10.2 us (3%)
    all_gather x1, waiting for transfers between devices, on_device(): lax.all_gather(local[0], 'replica', axis=0, tiled=True)  225 us
    all_to_all x1, blocking collectives, on_device(): lax.all_to_all(shards[0], 'tp', split_axis=1, concat_axis=0, tiled=True)  30.1 us
    all_gather x1, waiting for transfers between devices, on_device(): lax.all_gather(local[2], 'replica', axis=0, tiled=True)  25.1 us
    dot_general x3, matrix products, on_device(): jnp.dot(normed, piece, preferred_element_type=jnp.float32)  14.1 us
    all_to_all x1, blocking collectives, on_device(): lax.all_to_all(shards[1], 'tp', split_axis=1, concat_axis=0, tiled=True)  10 us
    all_to_all x1, blocking collectives, on_device(): lax.all_to_all(shards[2], 'tp', split_axis=1, concat_axis=0, tiled=True)  8.39 us
    all_gather x1, blocking collectives, on_device(): whole = lax.all_gather(hidden, 'tp', axis=2, tiled=True)  7.81 us
  transfers between devices with their start and end apart: 6, of which 3 were waited for; matrix products, arithmetic and copies ran while one was open for 8% of the time, Pallas kernels for 0%

commit v1 on v0

--- a/solution.py
+++ b/solution.py
@@ -10,6 +10,17 @@
 MOSTP = 8
 EPS = 1e-06
 THETA = 1000000.0
+
+
+def gather_around(x, axis, dim):
+    ways = lax.axis_size(axis)
+    pieces = [x]
+    for far in range(1, ways):
+        pieces.append(
+            lax.ppermute(pieces[far - 1], axis, [(d, (d - 1) % ways) for d in range(ways)])
+        )
+    line = jnp.concatenate(pieces, axis=dim)
+    return jnp.roll(line, lax.axis_index(axis) * x.shape[dim], axis=dim)
 
 
 def rotate(values, positions):
@@ -57,7 +68,7 @@
     pieces = (
         lax.all_gather(local[0], "replica", axis=0, tiled=True),
         lax.all_gather(local[1], "replica", axis=0, tiled=True),
-        lax.all_gather(local[2], "replica", axis=0, tiled=True),
+        gather_around(local[2], "replica", 0),
     )
     sums = tuple((jnp.dot(normed, piece, preferred_element_type=jnp.float32) for piece in pieces))
     made = [

time: 381 us -> 367 us (0.963)
  waiting for transfers between devices: 255 us -> 198 us
  starting transfers between devices: 10.2 us -> 40.8 us
  local copies, waits for them, and re-layouts: 23.1 us -> 39.6 us
  blocking collectives: 56.4 us -> 51.2 us
    all_gather x1, waiting for transfers between devices: 225 us -> 123 us  [on_device(): lax.all_gather(local[0], 'replica', axis=0, tiled=True)]
    ppermute x0 -> x7, waiting for transfers between devices: none -> 69.5 us  [gather_around(): lax.ppermute(pieces[far - 1], axis, [(d, (d - 1) % ways) for d in range(w...]
    ppermute x0 -> x7, starting transfers between devices: none -> 27.4 us  [gather_around(): lax.ppermute(pieces[far - 1], axis, [(d, (d - 1) % ways) for d in range(w...]
    all_gather x1 -> x0, waiting for transfers between devices: 25.1 us -> none  [on_device(): lax.all_gather(local[2], 'replica', axis=0, tiled=True)]
    unnamed x23 -> x46, local copies, waits for them, and re-layouts: 7.03 us -> 23.3 us
    all_to_all x1 -> x0, blocking collectives: 8.39 us -> none  [on_device(): lax.all_to_all(shards[2], 'tp', split_axis=1, concat_axis=0, tiled=True)]
  transfers between devices with their start and end apart: 6 -> 13, of which waited for: 3 -> 10; matrix products, arithmetic and copies ran while one was open for 8% -> 14% of each run, Pallas kernels for 0% -> 0%
where the time goes in v1:
time: 367 us; the launch traced here: 366 us
  waiting for transfers between devices  198 us (54%)
  blocking collectives  51.2 us (14%)
  starting transfers between devices  40.8 us (11%)
  local copies, waits for them, and re-layouts  39.6 us (11%)
  matrix products  19.3 us (5%)
  between operations  13.7 us (4%)
    all_gather x1, waiting for transfers between devices, on_device(): lax.all_gather(local[0], 'replica', axis=0, tiled=True)  123 us
    ppermute x7, waiting for transfers between devices, gather_around(): lax.ppermute(pieces[far - 1], axis, [(d, (d - 1) % ways) for d in range(w...  69.5 us
    all_to_all x1, blocking collectives, on_device(): lax.all_to_all(shards[0], 'tp', split_axis=1, concat_axis=0, tiled=True)  30.1 us
    ppermute x7, starting transfers between devices, gather_around(): lax.ppermute(pieces[far - 1], axis, [(d, (d - 1) % ways) for d in range(w...  27.4 us
    unnamed x46, local copies, waits for them, and re-layouts  23.3 us
    dot_general x3, matrix products, on_device(): jnp.dot(normed, piece, preferred_element_type=jnp.float32)  14.1 us
    all_gather x1, blocking collectives, on_device(): whole = lax.all_gather(hidden, 'tp', axis=2, tiled=True)  11.1 us
    all_to_all x1, blocking collectives, on_device(): lax.all_to_all(shards[1], 'tp', split_axis=1, concat_axis=0, tiled=True)  10 us
  transfers between devices with their start and end apart: 13, of which 10 were waited for; matrix products, arithmetic and copies ran while one was open for 14% of the time, Pallas kernels for 0%

profile of v1, /device:TPU:0, one launch (start us, length us, event | category | flops | bytes accessed | tf_op | source)
XLA Modules:
  0.0 365.9 jit_solution(17248176052459020156)
XLA Ops:
  7.9 10.0 %all_to_all.90 = bf16[256,4,128]{0,2,1:T(8,128)(2,1)S(1)} all-to-all(bf16[256,4,128]{0,2,1:T(8,128)(2,1)S(1)} %bitcast.103), channel_id=1, replica_groups=mesh['replica'=8,'tp'=4] {'tp'}, dimensions={1} | all-to-all | bytes 524288 | tf_op jit(solution)/shard_map/all_to_all | solution.py:65
  18.8 4.6 %copy.27 = bf16[256,4096]{0,1:T(8,128)(2,1)} copy(f32[256,4096]{1,0:T(8,128)} %param.16) | data formatting | bytes 6291456 | tf_op args[2]
  23.4 30.1 %all_to_all.91 = bf16[256,4,1024]{0,2,1:T(8,128)(2,1)} all-to-all(bf16[256,4,1024]{0,2,1:T(8,128)(2,1)} %bitcast.95), channel_id=1, replica_groups=mesh['replica'=8,'tp'=4] {'tp'}, dimensions={1} | all-to-all | bytes 4194304 | tf_op jit(solution)/shard_map/all_to_all | solution.py:64
  53.6 4.1 %copy.28 = bf16[4,256,1024]{2,1,0:T(8,128)(2,1)} copy(bf16[4,256,1024]{1,2,0:T(8,128)(2,1)} %bitcast.97) | data formatting | bytes 4194304 | tf_op jit(solution)/shard_map/all_to_all | solution.py:64
  58.5 3.4 all-to-all-start.4
  62.0 11.1 %all_gather.9 = bf16[12,4,8192]{2,1,0:T(4,128)(2,1)S(1)} all-gather(bf16[12,4,2048]{2,1,0:T(4,128)(2,1)S(1)} %copy-done.7), channel_id=1, replica_groups=mesh['replica'=8,'tp'=4] {'tp'}, dimensions={2}, use_global_device_ids=true | all-gather | bytes 983040 | tf_op jit(solution)/shard_map/all_gather | solution.py:54
  75.2 4.6 %collective-permute-start = (bf16[1024,128]{1,0:T(8,128)(2,1)S(1)}, bf16[1024,128]{1,0:T(8,128)(2,1)S(1)}, u32[]{:S(2)}, u32[]{:S(2)}) collective-permute-start(bf16[1024,128]{1,0:T(8,128)(2,1)S(1)} %bitcast.100), channel_id=1, source_target_pairs={{0,28},{4,0},{8,4},{12,8},{16,12},{20,16},{24,20},{28,24},{1,29},{... | collective-permute-start | bytes 786440 | tf_op jit(solution)/shard_map/ppermute | solution.py:20
  79.8 12.0 %collective-permute-done = bf16[1024,128]{1,0:T(8,128)(2,1)S(1)} collective-permute-done((bf16[1024,128]{1,0:T(8,128)(2,1)S(1)}, bf16[1024,128]{1,0:T(8,128)(2,1)S(1)}, u32[]{:S(2)}, u32[]{:S(2)}) %collective-permute-start) | collective-permute-done | bytes 262176 | tf_op jit(solution)/shard_map/ppermute | solution.py:20
  91.9 5.2 %collective-permute-start.1 = (bf16[1024,128]{1,0:T(8,128)(2,1)S(1)}, bf16[1024,128]{1,0:T(8,128)(2,1)S(1)}, u32[]{:S(2)}, u32[]{:S(2)}) collective-permute-start(bf16[1024,128]{1,0:T(8,128)(2,1)S(1)} %collective-permute-done), channel_id=1, source_target_pairs={{0,28},{4,0},{8,4},{12,8},{16,12},{20,16},{24,20},{28,24},{1,29},{... | collective-permute-start | bytes 786440 | tf_op jit(solution)/shard_map/ppermute | solution.py:20
  97.2 11.7 %collective-permute-done.1 = bf16[1024,128]{1,0:T(8,128)(2,1)S(1)} collective-permute-done((bf16[1024,128]{1,0:T(8,128)(2,1)S(1)}, bf16[1024,128]{1,0:T(8,128)(2,1)S(1)}, u32[]{:S(2)}, u32[]{:S(2)}) %collective-permute-start.1) | collective-permute-done | bytes 262176 | tf_op jit(solution)/shard_map/ppermute | solution.py:20
  108.9 5.2 %collective-permute-start.2 = (bf16[1024,128]{1,0:T(8,128)(2,1)S(1)}, bf16[1024,128]{1,0:T(8,128)(2,1)S(1)}, u32[]{:S(2)}, u32[]{:S(2)}) collective-permute-start(bf16[1024,128]{1,0:T(8,128)(2,1)S(1)} %collective-permute-done.1), channel_id=1, source_target_pairs={{0,28},{4,0},{8,4},{12,8},{16,12},{20,16},{24,20},{28,24},{1,29},{... | collective-permute-start | bytes 786440 | tf_op jit(solution)/shard_map/ppermute | solution.py:20
  114.1 11.5 %collective-permute-done.2 = bf16[1024,128]{1,0:T(8,128)(2,1)S(1)} collective-permute-done((bf16[1024,128]{1,0:T(8,128)(2,1)S(1)}, bf16[1024,128]{1,0:T(8,128)(2,1)S(1)}, u32[]{:S(2)}, u32[]{:S(2)}) %collective-permute-start.2) | collective-permute-done | bytes 262176 | tf_op jit(solution)/shard_map/ppermute | solution.py:20
  125.6 5.2 %collective-permute-start.3 = (bf16[1024,128]{1,0:T(8,128)(2,1)S(1)}, bf16[1024,128]{1,0:T(8,128)(2,1)}, u32[]{:S(2)}, u32[]{:S(2)}) collective-permute-start(bf16[1024,128]{1,0:T(8,128)(2,1)S(1)} %collective-permute-done.2), channel_id=1, source_target_pairs={{0,28},{4,0},{8,4},{12,8},{16,12},{20,16},{24,20},{28,24},{1,29},{... | collective-permute-start | bytes 786440 | tf_op jit(solution)/shard_map/ppermute | solution.py:20
  130.9 11.2 %collective-permute-done.3 = bf16[1024,128]{1,0:T(8,128)(2,1)} collective-permute-done((bf16[1024,128]{1,0:T(8,128)(2,1)S(1)}, bf16[1024,128]{1,0:T(8,128)(2,1)}, u32[]{:S(2)}, u32[]{:S(2)}) %collective-permute-start.3) | collective-permute-done | bytes 262176 | tf_op jit(solution)/shard_map/ppermute | solution.py:20
  142.1 5.3 %collective-permute-start.4 = (bf16[1024,128]{1,0:T(8,128)(2,1)}, bf16[1024,128]{1,0:T(8,128)(2,1)}, u32[]{:S(2)}, u32[]{:S(2)}) collective-permute-start(bf16[1024,128]{1,0:T(8,128)(2,1)} %collective-permute-done.3), channel_id=1, source_target_pairs={{0,28},{4,0},{8,4},{12,8},{16,12},{20,16},{24,20},{28,24},{1,29},{... | collective-permute-start | bytes 786440 | tf_op jit(solution)/shard_map/ppermute | solution.py:20
  149.0 2.8 gather_fusion.1
  151.8 4.3 %gather_fusion = bf16[24,4,128,128]{3,2,1,0:T(8,128)(2,1)} fusion(bf16[16,4,128,128]{3,2,1,0:T(8,128)(2,1)} %param.23, s32[1024]{0:T(1024)S(1)} %pad_clamp_fusion), kind=kCustom, calls=%fused_computation.clone | custom fusion | bytes 6291552 | tf_op jit(solution)/shard_map/jit(_take)/gather | solution.py:95
  157.0 5.1 %collective-permute-done.4 = bf16[1024,128]{1,0:T(8,128)(2,1)} collective-permute-done((bf16[1024,128]{1,0:T(8,128)(2,1)}, bf16[1024,128]{1,0:T(8,128)(2,1)}, u32[]{:S(2)}, u32[]{:S(2)}) %collective-permute-start.4) | collective-permute-done | bytes 262176 | tf_op jit(solution)/shard_map/ppermute | solution.py:20
  162.1 1.9 collective-permute-start.5
  166.4 1.7 constant_dynamic-update-slice_fusion.12
  168.1 14.3 %collective-permute-done.5 = bf16[1024,128]{1,0:T(8,128)(2,1)S(1)} collective-permute-done((bf16[1024,128]{1,0:T(8,128)(2,1)}, bf16[1024,128]{1,0:T(8,128)(2,1)S(1)}, u32[]{:S(2)}, u32[]{:S(2)}) %collective-permute-start.5) | collective-permute-done | bytes 262176 | tf_op jit(solution)/shard_map/ppermute | solution.py:20
  186.4 3.7 %collective-permute-done.6 = bf16[1024,128]{1,0:T(8,128)(2,1)S(1)} collective-permute-done((bf16[1024,128]{1,0:T(8,128)(2,1)S(1)}, bf16[1024,128]{1,0:T(8,128)(2,1)S(1)}, u32[]{:S(2)}, u32[]{:S(2)}) %collective-permute-start.6) | collective-permute-done | bytes 262176 | tf_op jit(solution)/shard_map/ppermute | solution.py:20
  193.7 1.7 constant_dynamic-update-slice_fusion.3
  198.5 2.7 fusion.29
  201.1 3.3 all-to-all-start.3
  204.4 2.7 fusion.30
  208.2 123.1 %all-gather.3.cloned.1.call-done = bf16[8192,1024]{1,0:T(8,128)(2,1)} async-done(((bf16[1024,1024]{1,0:T(8,128)(2,1)}), bf16[8192,1024]{1,0:T(8,128)(2,1)}) %all-gather.3.cloned.1.call-update) | async-done | bytes 16777232 | tf_op jit(solution)/shard_map/all_gather | solution.py:69
  331.3 8.8 %fusion.21 = bf16[48,1024]{1,0:T(8,128)(2,1)S(1)} fusion(bf16[48,8192]{1,0:T(8,128)(2,1)S(1)} %reshape.170, bf16[8192,1024]{1,0:T(8,128)(2,1)} %all-gather.3.cloned.1.call-done, f32[1024]{0:T(1024)S(1)} %copy-done.10), kind=kOutput, calls=%fused_computation.29 | convolution fusion | flops 805404672 | bytes 17666048 | tf_op jit(solution)/shard_map/dot_general | solution.py:73
  340.8 3.3 all-to-all-start.1
  344.2 4.2 %all-to-all-done.1 = bf16[12,4,1024]{2,1,0:T(4,128)(2,1)S(1)} async-done(((bf16[12,4,1024]{2,1,0:T(4,128)(2,1)}), bf16[12,4,1024]{2,1,0:T(4,128)(2,1)S(1)}, u32[]{:S(2)}, u32[]{:S(2)}) %all-to-all-start.1) | async-done | bytes 98336 | tf_op jit(solution)/shard_map/all_to_all | solution.py:79
  348.4 3.4 all-to-all-start.5
  353.0 3.4 bitcast_reduce_fusion
  (89 shorter events, 26.8 us)
Async XLA Ops:
  6.5 142.5 %copy-start = (bf16[16,4,128,128]{3,2,1,0:T(8,128)(2,1)S(1)}, bf16[16,4,128,128]{3,2,1,0:T(8,128)(2,1)}, u32[]{:S(2)}) copy-start(bf16[16,4,128,128]{3,2,1,0:T(8,128)(2,1)} %param.22) | copy-start | bytes 6291460
  6.5 191.9 %all-gather.5.cloned.1.call-start = ((), (), s32[]{:S(2)}) async-start(), calls=%async_computation.7 | async-start | bytes 2359296 | tf_op jit(solution)/shard_map/all_gather | solution.py:70
  18.8 312.6 %all-gather.3.cloned.1.call-start = ((), (), s32[]{:S(2)}) async-start(), calls=%async_computation.6 | async-start | bytes 18874368 | tf_op jit(solution)/shard_map/all_gather | solution.py:69
  53.6 4.1 %copy-start.6 = (f32[256,512]{1,0:T(8,128)S(1)}, f32[256,512]{1,0:T(8,128)}, u32[]{:S(2)}) copy-start(f32[256,512]{1,0:T(8,128)} %param.18) | copy-start | bytes 1572868
  53.6 8.4 %copy-start.7 = (bf16[12,4,2048]{2,1,0:T(4,128)(2,1)S(1)}, bf16[12,4,2048]{2,1,0:T(4,128)(2,1)}, u32[]{:S(2)}) copy-start(bf16[12,4,2048]{2,1,0:T(4,128)(2,1)} %param.14) | copy-start | bytes 589828
  57.6 15.9 %copy-start.8 = (f32[8192]{0:T(1024)S(1)}, f32[8192]{0:T(1024)}, u32[]{:S(2)}) copy-start(f32[8192]{0:T(1024)} %param.15) | copy-start | bytes 98308
  57.7 17.3 %copy-start.11 = (s32[3]{0:T(128)S(1)}, s32[3]{0:T(128)}, u32[]{:S(2)}) copy-start(s32[3]{0:T(128)} %param.24) | copy-start | bytes 40
  57.7 22.1 %copy-start.9 = (s32[3,8]{1,0:T(4,128)S(1)}, s32[3,8]{1,0:T(4,128)}, u32[]{:S(2)}) copy-start(s32[3,8]{1,0:T(4,128)} %param.25) | copy-start | bytes 292
  58.5 16.5 %all-to-all-start.4 = ((bf16[256,4,128]{0,2,1:T(8,128)(2,1)}), bf16[256,4,128]{0,2,1:T(8,128)(2,1)S(1)}, u32[]{:S(2)}, u32[]{:S(2)}) async-start(bf16[256,4,128]{0,2,1:T(8,128)(2,1)} %bitcast.27), calls=%async_computation.4 | async-start | bytes 524288 | tf_op jit(solution)/shard_map/all_to_all | solution.py:66
  75.2 16.7 %collective-permute-start = (bf16[1024,128]{1,0:T(8,128)(2,1)S(1)}, bf16[1024,128]{1,0:T(8,128)(2,1)S(1)}, u32[]{:S(2)}, u32[]{:S(2)}) collective-permute-start(bf16[1024,128]{1,0:T(8,128)(2,1)S(1)} %bitcast.100), channel_id=1, source_target_pairs={{0,28},{4,0},{8,4},{12,8},{16,12},{20,16},{24,20},{28,24},{1,29},{... | collective-permute-start | bytes 786440 | tf_op jit(solution)/shard_map/ppermute | solution.py:20
  91.9 17.0 %collective-permute-start.1 = (bf16[1024,128]{1,0:T(8,128)(2,1)S(1)}, bf16[1024,128]{1,0:T(8,128)(2,1)S(1)}, u32[]{:S(2)}, u32[]{:S(2)}) collective-permute-start(bf16[1024,128]{1,0:T(8,128)(2,1)S(1)} %collective-permute-done), channel_id=1, source_target_pairs={{0,28},{4,0},{8,4},{12,8},{16,12},{20,16},{24,20},{28,24},{1,29},{... | collective-permute-start | bytes 786440 | tf_op jit(solution)/shard_map/ppermute | solution.py:20
  108.9 38.6 %copy-start.2 = (bf16[1024,128]{1,0:T(8,128)(2,1)}, bf16[1024,128]{1,0:T(8,128)(2,1)S(1)}, u32[]{:S(2)}) copy-start(bf16[1024,128]{1,0:T(8,128)(2,1)S(1)} %collective-permute-done.1) | copy-start | bytes 786436
  108.9 16.8 %collective-permute-start.2 = (bf16[1024,128]{1,0:T(8,128)(2,1)S(1)}, bf16[1024,128]{1,0:T(8,128)(2,1)S(1)}, u32[]{:S(2)}, u32[]{:S(2)}) collective-permute-start(bf16[1024,128]{1,0:T(8,128)(2,1)S(1)} %collective-permute-done.1), channel_id=1, source_target_pairs={{0,28},{4,0},{8,4},{12,8},{16,12},{20,16},{24,20},{28,24},{1,29},{... | collective-permute-start | bytes 786440 | tf_op jit(solution)/shard_map/ppermute | solution.py:20
  125.6 21.8 %copy-start.4 = (bf16[1024,128]{1,0:T(8,128)(2,1)}, bf16[1024,128]{1,0:T(8,128)(2,1)S(1)}, u32[]{:S(2)}) copy-start(bf16[1024,128]{1,0:T(8,128)(2,1)S(1)} %collective-permute-done.2) | copy-start | bytes 786436
  125.6 16.5 %collective-permute-start.3 = (bf16[1024,128]{1,0:T(8,128)(2,1)S(1)}, bf16[1024,128]{1,0:T(8,128)(2,1)}, u32[]{:S(2)}, u32[]{:S(2)}) collective-permute-start(bf16[1024,128]{1,0:T(8,128)(2,1)S(1)} %collective-permute-done.2), channel_id=1, source_target_pairs={{0,28},{4,0},{8,4},{12,8},{16,12},{20,16},{24,20},{28,24},{1,29},{... | collective-permute-start | bytes 786440 | tf_op jit(solution)/shard_map/ppermute | solution.py:20
  142.1 19.9 %collective-permute-start.4 = (bf16[1024,128]{1,0:T(8,128)(2,1)}, bf16[1024,128]{1,0:T(8,128)(2,1)}, u32[]{:S(2)}, u32[]{:S(2)}) collective-permute-start(bf16[1024,128]{1,0:T(8,128)(2,1)} %collective-permute-done.3), channel_id=1, source_target_pairs={{0,28},{4,0},{8,4},{12,8},{16,12},{20,16},{24,20},{28,24},{1,29},{... | collective-permute-start | bytes 786440 | tf_op jit(solution)/shard_map/ppermute | solution.py:20
  156.2 36.1 %copy-start.3 = (bf16[1024,128]{1,0:T(8,128)(2,1)S(1)}, bf16[1024,128]{1,0:T(8,128)(2,1)}, u32[]{:S(2)}) copy-start(bf16[1024,128]{1,0:T(8,128)(2,1)} %copy-done.2) | copy-start | bytes 786436
  156.2 36.8 %copy-start.5 = (bf16[1024,128]{1,0:T(8,128)(2,1)S(1)}, bf16[1024,128]{1,0:T(8,128)(2,1)}, u32[]{:S(2)}) copy-start(bf16[1024,128]{1,0:T(8,128)(2,1)} %copy-done.4) | copy-start | bytes 786436
  162.1 20.3 %collective-permute-start.5 = (bf16[1024,128]{1,0:T(8,128)(2,1)}, bf16[1024,128]{1,0:T(8,128)(2,1)S(1)}, u32[]{:S(2)}, u32[]{:S(2)}) collective-permute-start(bf16[1024,128]{1,0:T(8,128)(2,1)} %collective-permute-done.4), channel_id=1, source_target_pairs={{0,28},{4,0},{8,4},{12,8},{16,12},{20,16},{24,20},{28,24},{1,29},{... | collective-permute-start | bytes 786440 | tf_op jit(solution)/shard_map/ppermute | solution.py:20
  168.1 30.4 %copy-start.12 = (f32[128]{0:T(128)S(1)}, f32[128]{0:T(128)}, u32[]{:S(2)}) copy-start(f32[128]{0:T(128)} %param.20) | copy-start | bytes 1540
  182.4 7.7 %collective-permute-start.6 = (bf16[1024,128]{1,0:T(8,128)(2,1)S(1)}, bf16[1024,128]{1,0:T(8,128)(2,1)S(1)}, u32[]{:S(2)}, u32[]{:S(2)}) collective-permute-start(bf16[1024,128]{1,0:T(8,128)(2,1)S(1)} %collective-permute-done.5), channel_id=1, source_target_pairs={{0,28},{4,0},{8,4},{12,8},{16,12},{20,16},{24,20},{28,24},{1,29},{... | collective-permute-start | bytes 786440 | tf_op jit(solution)/shard_map/ppermute | solution.py:20
  192.2 12.2 %copy-start.13 = (f32[128]{0:T(128)S(1)}, f32[128]{0:T(128)}, u32[]{:S(2)}) copy-start(f32[128]{0:T(128)} %param.21) | copy-start | bytes 1540
  197.8 133.6 %copy-start.10 = (f32[1024]{0:T(1024)S(1)}, f32[1024]{0:T(1024)}, u32[]{:S(2)}) copy-start(f32[1024]{0:T(1024)} %param.19) | copy-start | bytes 12292
  201.1 7.1 %all-to-all-start.3 = ((bf16[12,4,128]{2,1,0:T(4,128)(2,1)}), bf16[12,4,128]{2,1,0:T(4,128)(2,1)S(1)}, u32[]{:S(2)}, u32[]{:S(2)}) async-start(bf16[12,4,128]{2,1,0:T(4,128)(2,1)} %bitcast.19), calls=%async_computation.3 | async-start | bytes 24576 | tf_op jit(solution)/shard_map/all_to_all | solution.py:80
  340.8 7.6 %all-to-all-start.1 = ((bf16[12,4,1024]{2,1,0:T(4,128)(2,1)}), bf16[12,4,1024]{2,1,0:T(4,128)(2,1)S(1)}, u32[]{:S(2)}, u32[]{:S(2)}) async-start(bf16[12,4,1024]{2,1,0:T(4,128)(2,1)} %reshape.171), calls=%async_computation.1 | async-start | bytes 196608 | tf_op jit(solution)/shard_map/all_to_all | solution.py:79
  348.4 9.6 %all-to-all-start.5 = ((bf16[12,4,128]{2,1,0:T(4,128)(2,1)}), bf16[12,4,128]{2,1,0:T(4,128)(2,1)S(1)}, u32[]{:S(2)}, u32[]{:S(2)}) async-start(bf16[12,4,128]{2,1,0:T(4,128)(2,1)} %bitcast.30), calls=%async_computation.5 | async-start | bytes 24576 | tf_op jit(solution)/shard_map/all_to_all | solution.py:81
  353.0 4.0 %copy-start.1 = (bf16[24,4,128,128]{3,2,1,0:T(8,128)(2,1)S(1)}, bf16[24,4,128,128]{3,2,1,0:T(8,128)(2,1)}, u32[]{:S(2)}) copy-start(bf16[24,4,128,128]{3,2,1,0:T(8,128)(2,1)} %gather_fusion) | copy-start | bytes 9437188
Sparse Core Ops, SparseCore 0:
  18.9 49.3 all-gather.4
  70.5 260.8 all-gather.2
